TPU v7x, 32 devices: a whole 2x2x4 slice. The times are simulated.
32 devices in a mesh: dp: 2 (over y), expert: 16 (over z, x, core).
Axes of the slice: x: 2, y: 2, z: 4, core: 2. Of those that a mesh axis runs over, the one named last changes fastest.
Arguments:
- soft_tokens: bfloat16 [2048, 2048], P('expert', 'dp'), may hold values from -6 to 6
- expert_ids: int32 [2048, 8], P('expert'), may hold values from 0 to 31, all different within a row; in each aligned block of 128 rows (0 to 127, 128 to 255, ...) at most 40 rows name the same one
- gate_mix: float32 [2048, 8], P('expert'), may hold values from 0.05 to 0.35
- w_gate: bfloat16 [32, 2048, 768], P('expert', 'dp'), may hold values from -0.125 to 0.125
- w_up: bfloat16 [32, 2048, 768], P('expert', 'dp'), may hold values from -0.125 to 0.125
- w_down: bfloat16 [32, 768, 2048], P('expert', None, 'dp'), may hold values from -0.21875 to 0.21875
- out_grad: bfloat16 [2048, 2048], P('expert', 'dp'), may hold values from -6 to 6
Outputs:
- mixed: bfloat16 [2048, 2048], P('expert', 'dp')
- token_grad: bfloat16 [2048, 2048], P('expert', 'dp')
Inputs may be any that keep to these rules, and one draw needn't show every extreme that they name: `expert_ids`: each row names 8 different experts. Among the 128 rows of one device no expert is named by more than 40 rows, and in some device one expert is named by exactly 40 rows.
All inputs are finite; a program needn't handle non-finite values.
Results may differ from a plain program's by a relative error of at most 0.023.
Values may be sent and summed in bfloat16 or wider, within the bound.
A program may use at most 128 MiB of HBM per device.

v0:
```python
import functools

import jax
import jax.numpy as jnp
from jax import lax
from jax.experimental import pallas as pl
from jax.experimental.pallas import tpu as pltpu
from jax.sharding import PartitionSpec as P

F32 = jnp.float32
BF16 = jnp.bfloat16


def slot_maps(ids, mix, first, local_experts, capacity):
    tok_rows = ids.shape[1]
    own = first + jnp.arange(local_experts, dtype=jnp.int32)
    hit = ids[:, None, :, :] == own[None, :, None, None]
    named = jnp.any(hit, axis=3)
    weight = jnp.sum(jnp.where(hit, mix[:, None, :, :], 0.0), axis=3)
    before = jnp.arange(tok_rows)[:, None] < jnp.arange(tok_rows)[None, :]
    place = jnp.einsum(
        "set,tu->seu", named.astype(BF16), before.astype(BF16), preferred_element_type=F32
    ).astype(jnp.int32)
    slots = jnp.arange(capacity, dtype=jnp.int32)
    pick = (place[:, :, None, :] == slots[None, None, :, None]) & named[:, :, None, :]
    slot_weight = jnp.sum(jnp.where(pick, weight[:, :, None, :], 0.0), axis=3)
    return pick.astype(BF16), slot_weight


def per_device(soft_tokens, expert_ids, gate_mix, w_gate, w_up, w_down, out_grad):
    tok_rows, width_part = soft_tokens.shape
    top_count = expert_ids.shape[1]
    local_experts = w_gate.shape[0]
    hidden = w_gate.shape[2]
    groups = lax.axis_size("expert")
    dp_count = lax.axis_size("dp")
    experts = groups * local_experts
    capacity = max(2, tok_rows * top_count * 5 // (4 * experts))
    both = lax.all_gather(jnp.concatenate([soft_tokens, out_grad], axis=1), "expert")
    ids = lax.all_gather(expert_ids, "expert")
    mix = lax.all_gather(gate_mix, "expert")
    first = lax.axis_index("expert") * local_experts
    pick, slot_weight = slot_maps(ids, mix, first, local_experts, capacity)
    rows = jnp.einsum("sect,std->secd", pick, both, preferred_element_type=F32).astype(BF16)
    pre = [
        jnp.einsum("secd,edf->secf", rows[..., :width_part], w, preferred_element_type=F32)
        for w in (w_gate, w_up)
    ]
    back = jnp.einsum("secd,efd->secf", rows[..., width_part:], w_down, preferred_element_type=F32)
    part = jnp.concatenate(pre + [back], axis=-1).astype(BF16)
    total = part.astype(F32)
    moved = part
    for _ in range(dp_count - 1):
        moved = lax.ppermute(moved, "dp", [(i, (i + 1) % dp_count) for i in range(dp_count)])
        total = total + moved.astype(F32)
    a = total[..., :hidden]
    b = total[..., hidden : 2 * hidden]
    back = total[..., 2 * hidden :] * slot_weight[..., None]
    sig = jax.nn.sigmoid(a)
    act = (a * sig * b * slot_weight[..., None]).astype(BF16)
    d_gate = (back * b * sig * (1.0 + a * (1.0 - sig))).astype(BF16)
    d_up = (back * a * sig).astype(BF16)
    out = jnp.einsum("secf,efd->secd", act, w_down, preferred_element_type=F32)
    grad = jnp.einsum("secf,edf->secd", d_gate, w_gate, preferred_element_type=F32) + jnp.einsum(
        "secf,edf->secd", d_up, w_up, preferred_element_type=F32
    )
    result = jnp.concatenate([out, grad], axis=-1).astype(BF16)
    spread = jnp.einsum("sect,secd->std", pick, result, preferred_element_type=F32).astype(BF16)
    summed = lax.psum_scatter(spread, "expert", scatter_dimension=0, tiled=False)
    return summed[:, :width_part], summed[:, width_part:]


MESH = pl.DeviceIdType.MESH
MID = 2
CORES = 2


def flip(value, step, count):
    out, bit = 0, 1
    while bit < count:
        out = out + lax.rem(lax.div(value, bit) + lax.div(step, bit), 2) * bit
        bit *= 2
    return out


def fused_kernel(
    groups, x_ref, meta_ref, wg_ref, wu_ref, wd_ref, mixed_ref, tgrad_ref,
    ag, metas, psend, precv, acc, crecv, xsend, xrecv, zsend, zrecv,
    ms, mr, zs, zr, xs, xr, cs, cr, ys, yr, rcs, rcr, rxs, rxr, rzs, rzr,
):
    rows, wide = x_ref.shape
    half = wide // 2
    experts, _, hid = wg_ref.shape
    plane = MID * CORES
    outer = groups // plane
    slots = psend.shape[2]
    me = lax.axis_index("expert")
    y = lax.axis_index("dp")
    z = lax.div(me, plane)
    x = lax.rem(lax.div(me, CORES), MID)
    c = lax.rem(me, CORES)
    core_peer = (z * MID + x) * CORES + 1 - c
    x_peer = (z * MID + 1 - x) * CORES + c

    def at(expert):
        return {"dp": y, "expert": expert}

    def copy(src, dst, send, recv, device):
        return pltpu.make_async_remote_copy(
            src_ref=src, dst_ref=dst, send_sem=send, recv_sem=recv,
            device_id=device, device_id_type=MESH,
        )

    barrier = pltpu.get_barrier_semaphore()
    for k in range(1, groups):
        pl.semaphore_signal(
            barrier, inc=1, device_id=at(lax.rem(me + k, groups)), device_id_type=MESH
        )
    other_dp = {"dp": 1 - y, "expert": me}
    pl.semaphore_signal(barrier, inc=1, device_id=other_dp, device_id_type=MESH)
    pl.semaphore_wait(barrier, groups)

    def meta_copy(k):
        to = lax.rem(me + k, groups)
        return copy(meta_ref.at[to], metas.at[me], ms.at[k], mr.at[k], at(to))

    def meta_arrival(k):
        source = lax.rem(me + groups - k, groups)
        return copy(meta_ref.at[source], metas.at[source], ms.at[k], mr.at[k], at(source))

    def peer_of(step):
        return (flip(z, step, outer) * MID + x) * CORES + c

    def z_copy(step):
        return copy(x_ref, ag.at[me], zs.at[step], zr.at[step], at(peer_of(step)))

    def z_arrival(step):
        blk = peer_of(step)
        return copy(x_ref, ag.at[blk], zs.at[step], zr.at[step], at(blk))

    def x_copy(step, blk):
        return copy(ag.at[blk], ag.at[blk], xs.at[step], xr.at[step], at(x_peer))

    def c_copy(step, which, blk):
        return copy(
            ag.at[blk], ag.at[blk], cs.at[step, which], cr.at[step, which], at(core_peer)
        )

    def y_copy(step, e):
        return copy(
            psend.at[step, e], precv.at[step, e], ys.at[step, e], yr.at[step, e], other_dp
        )

    def rc_copy(step, part, across):
        return copy(
            acc.at[part, across * CORES + 1 - c], crecv.at[step, part, across],
            rcs.at[step, part, across], rcr.at[step, part, across], at(core_peer),
        )

    def rx_copy(step, part):
        return copy(
            xsend.at[part], xrecv.at[step, part],
            rxs.at[step, part], rxr.at[step, part], at(x_peer),
        )

    def rz_copy(step, part):
        return copy(
            zsend.at[step, part], zrecv.at[step, part],
            rzs.at[step, part], rzr.at[step, part], at(peer_of(step)),
        )

    ag[me] = x_ref[...]
    metas[me] = meta_ref[me]
    for k in range(1, groups):
        meta_copy(k).start()
    for i in range(1, outer):
        z_copy(outer - i).start()

    def dot(a, b, dims):
        return lax.dot_general(a, b, (dims, ((), ())), preferred_element_type=jnp.float32)

    def pick_of(p):
        tiles = metas[pl.ds(p * plane, plane)]
        line = jnp.concatenate([tiles[b] for b in range(plane)], axis=1)
        slot = lax.broadcasted_iota(jnp.int32, (slots, plane * rows), 0).astype(jnp.float32)
        picks, weights = [], []
        for e in range(experts):
            match = slot == line[e : e + 1]
            picks.append(jnp.where(match, 1.0, 0.0))
            weights.append(
                jnp.sum(
                    jnp.where(match, line[experts + e : experts + e + 1], 0.0),
                    axis=1, keepdims=True,
                )
            )
        return jnp.concatenate(picks, axis=0), weights

    def first_half(i):
        step = lax.rem(outer - i, outer)
        p = flip(z, step, outer)
        mine = (p * MID + x) * CORES + c
        across = (p * MID + 1 - x) * CORES + c

        @pl.when(i > 0)
        def _():
            z_arrival(step).wait_recv()

        x_copy(step, mine).start()
        c_copy(step, 0, mine).start()

        @pl.when(i == 0)
        def _():
            @pl.loop(1, groups)
            def _(k):
                meta_arrival(k).wait_recv()

        x_copy(step, across).wait_recv()
        c_copy(step, 1, across).start()
        c_copy(step, 0, mine + 1 - 2 * c).wait_recv()
        c_copy(step, 1, across + 1 - 2 * c).wait_recv()
        pick, _ = pick_of(p)
        pick = pick.astype(BF16)
        block = ag[pl.ds(p * plane, plane)].reshape(plane * rows, wide)
        for e in range(experts):
            got = dot(pick[e * slots : (e + 1) * slots], block, ((1,), (0,))).astype(BF16)
            tok, cot = got[:, :half], got[:, half:]
            psend[step, e, :, :hid] = dot(tok, wg_ref[e], ((1,), (0,))).astype(BF16)
            psend[step, e, :, hid : 2 * hid] = dot(tok, wu_ref[e], ((1,), (0,))).astype(BF16)
            psend[step, e, :, 2 * hid :] = dot(cot, wd_ref[e], ((1,), (1,))).astype(BF16)
            y_copy(step, e).start()

    def second_half(i):
        step = lax.rem(outer - i, outer)
        p = flip(z, step, outer)
        pick, weights = pick_of(p)
        spread_by = pick.T.astype(BF16)
        outs, changes = [], []
        for e in range(experts):
            y_copy(step, e).wait_recv()

            def total(lo):
                part = psend[step, e, :, lo : lo + hid].astype(F32)
                return part + precv[step, e, :, lo : lo + hid].astype(F32)

            a, b = total(0), total(hid)
            back = total(2 * hid) * weights[e]
            sig = jax.nn.sigmoid(a)
            silu = a * sig
            act = (silu * b * weights[e]).astype(BF16)
            d_gate = (back * b * sig * (1.0 + a * (1.0 - sig))).astype(BF16)
            changes.append((d_gate, (back * silu).astype(BF16)))
            outs.append(dot(act, wd_ref[e], ((1,), (0,))).astype(BF16))

        def scatter(part, values):
            rows_out = dot(spread_by, jnp.concatenate(values, axis=0), ((1,), (0,)))
            acc[part] = rows_out.astype(BF16).reshape(plane, rows, half)
            for m in range(MID):
                rc_copy(step, part, m).start()

        scatter(0, outs)
        grads = [
            (
                dot(changes[e][0], wg_ref[e], ((1,), (1,)))
                + dot(changes[e][1], wu_ref[e], ((1,), (1,)))
            ).astype(BF16)
            for e in range(experts)
        ]

        def to_x_peer(part):
            for m in range(MID):
                rc_copy(step, part, m).wait_recv()
            there = acc[part, (1 - x) * CORES + c].astype(F32)
            xsend[part] = (there + crecv[step, part, 1 - x].astype(F32)).astype(BF16)
            rx_copy(step, part).start()

        def to_owner(part):
            here = acc[part, x * CORES + c].astype(F32) + crecv[step, part, x].astype(F32)
            rx_copy(step, part).wait_recv()
            here = (here + xrecv[step, part].astype(F32)).astype(BF16)

            @pl.when(i == 0)
            def _():
                zrecv[0, part] = here

            @pl.when(i > 0)
            def _():
                zsend[step, part] = here
                rz_copy(step, part).start()

        to_x_peer(0)
        scatter(1, grads)
        to_x_peer(1)
        to_owner(0)
        to_owner(1)
        for part in range(2):
            rx_copy(step, part).wait_send()
            for m in range(MID):
                rc_copy(step, part, m).wait_send()

    ahead = 2

    @pl.loop(0, outer + ahead)
    def _(i):
        @pl.when(i < outer)
        def _():
            first_half(i)

        @pl.when(i >= ahead)
        def _():
            second_half(i - ahead)

    @pl.loop(1, groups)
    def _(k):
        meta_copy(k).wait_send()

    for step in range(outer):
        x_copy(step, me).wait_send()
        c_copy(step, 0, me).wait_send()
        c_copy(step, 1, me).wait_send()
        for e in range(experts):
            y_copy(step, e).wait_send()
    for step in range(1, outer):
        z_copy(step).wait_send()
    for part, out_ref in enumerate((mixed_ref, tgrad_ref)):
        final = zrecv[0, part].astype(F32)
        for step in range(1, outer):
            rz_copy(step, part).wait_recv()
            final = final + zrecv[step, part].astype(F32)
        out_ref[...] = final.astype(BF16)
    for step in range(1, outer):
        for part in range(2):
            rz_copy(step, part).wait_send()


def fused_device(soft_tokens, expert_ids, gate_mix, w_gate, w_up, w_down, out_grad):
    tok_rows, width_part = soft_tokens.shape
    top_count = expert_ids.shape[1]
    local_experts, _, hid = w_gate.shape
    groups = lax.axis_size("expert")
    experts = groups * local_experts
    capacity = max(2, tok_rows * top_count * 5 // (4 * experts))
    plane = MID * CORES
    outer = groups // plane
    wide = 2 * width_part
    ids, mix = expert_ids.T, gate_mix.T
    hit = ids[None] == jnp.arange(experts, dtype=jnp.int32)[:, None, None]
    named = jnp.any(hit, axis=1)
    weight = jnp.sum(jnp.where(hit, mix[None], 0.0), axis=1)
    before = jnp.arange(tok_rows)[:, None] < jnp.arange(tok_rows)[None, :]
    place = jnp.dot(named.astype(BF16), before.astype(BF16), preferred_element_type=F32)
    offset = (lax.axis_index("expert") % plane * capacity).astype(F32)
    key = jnp.where(named, place + offset, -1.0)
    shape = (groups, local_experts, tok_rows)
    meta = jnp.concatenate([key.reshape(shape), weight.reshape(shape)], axis=1)
    meta = jnp.pad(meta, ((0, 0), (0, -2 * local_experts % 8), (0, 0)))
    both = jnp.concatenate([soft_tokens, out_grad], axis=1)
    slots = plane * capacity
    vmem = pl.BlockSpec(memory_space=pltpu.VMEM)
    dma = pltpu.SemaphoreType.DMA
    out = jax.ShapeDtypeStruct((tok_rows, width_part), BF16)
    return pl.pallas_call(
        functools.partial(fused_kernel, groups),
        out_shape=(out, out),
        in_specs=[vmem] * 5,
        out_specs=(vmem, vmem),
        scratch_shapes=[
            pltpu.VMEM((groups, tok_rows, wide), BF16),
            pltpu.VMEM(meta.shape, F32),
            pltpu.VMEM((outer, local_experts, slots, 3 * hid), BF16),
            pltpu.VMEM((outer, local_experts, slots, 3 * hid), BF16),
            pltpu.VMEM((2, plane, tok_rows, width_part), BF16),
            pltpu.VMEM((outer, 2, MID, tok_rows, width_part), BF16),
            pltpu.VMEM((2, tok_rows, width_part), BF16),
            pltpu.VMEM((outer, 2, tok_rows, width_part), BF16),
            pltpu.VMEM((outer, 2, tok_rows, width_part), BF16),
            pltpu.VMEM((outer, 2, tok_rows, width_part), BF16),
            dma((groups,)), dma((groups,)),
            dma((outer,)), dma((outer,)),
            dma((outer,)), dma((outer,)),
            dma((outer, MID)), dma((outer, MID)),
            dma((outer, local_experts)), dma((outer, local_experts)),
            dma((outer, 2, MID)), dma((outer, 2, MID)),
            dma((outer, 2)), dma((outer, 2)),
            dma((outer, 2)), dma((outer, 2)),
        ],
        compiler_params=pltpu.CompilerParams(
            collective_id=0, has_side_effects=True, vmem_limit_bytes=67043328
        ),
    )(both, meta, w_gate, w_up, w_down)


def solution(mesh):
    in_specs = (
        P("expert", "dp"),
        P("expert", None),
        P("expert", None),
        P("expert", "dp", None),
        P("expert", "dp", None),
        P("expert", None, "dp"),
        P("expert", "dp"),
    )
    out_specs = (P("expert", "dp"), P("expert", "dp"))
    fits = mesh.shape["dp"] == 2 and mesh.shape["expert"] in (4, 8, 16)
    return jax.shard_map(
        fused_device if fits else per_device,
        mesh=mesh, in_specs=in_specs, out_specs=out_specs, check_vma=False,
    )
```

profile of v0, /device:TPU:0, one launch (start us, length us, event | category | flops | bytes accessed | tf_op | source)
XLA Modules:
  0.0 201.4 jit_solution(14561121773162562701)
XLA Ops:
  0.6 0.7 fusion.1
  1.4 0.1 fusion
  1.5 0.8 select_reduce_fusion
  2.3 0.7 select_maximum_fusion.meta_ref
  2.9 1.9 pad_maximum_fusion.x_ref
  4.8 193.3 %shard_map.86 = (bf16[128,1024]{1,0:T(8,128)(2,1)}, bf16[128,1024]{1,0:T(8,128)(2,1)}) custom-call(bf16[128,2048]{1,0:T(8,128)(2,1)} %pad_maximum_fusion.x_ref, f32[16,8,128]{2,1,0:T(8,128)} %select_maximum_fusion.meta_ref, bf16[2,1024,768]{2,1,0:T(8,128)(2,1)} %wg_ref.1, bf16[2,1024,768]{2,1,0:T(8,128)(2,1)} %wu_ref.1, bf16[2,768,1024]{2,1,0:T(8,128)(2,1)} %wd_ref.1), custom_call_target="tpu_custom_call" | custom-call | tf_op jit(solution)/shard_map/pallas_call | solution.py:361
  198.1 1.7 copy.11
  199.8 1.7 copy.12
where the time goes:
time: 202 us; the launch traced here: 201 us
  Pallas kernels  193 us (96%)
  other arithmetic  4 us (2%)
  local copies, waits for them, and re-layouts  3.34 us (2%)
    pallas_call x1, Pallas kernels, fused_device(): pl.pallas_call(functools.partial(fused_kernel, groups), out_shape=(out, o...  193 us

commit v1 on v0

v1 whole, which is shorter than its diff:
```python
import functools

import jax
import jax.numpy as jnp
from jax import lax
from jax.experimental import pallas as pl
from jax.experimental.pallas import tpu as pltpu
from jax.sharding import PartitionSpec as P

F32 = jnp.float32
BF16 = jnp.bfloat16


def slot_maps(ids, mix, first, local_experts, capacity):
    tok_rows = ids.shape[1]
    own = first + jnp.arange(local_experts, dtype=jnp.int32)
    hit = ids[:, None, :, :] == own[None, :, None, None]
    named = jnp.any(hit, axis=3)
    weight = jnp.sum(jnp.where(hit, mix[:, None, :, :], 0.0), axis=3)
    before = jnp.arange(tok_rows)[:, None] < jnp.arange(tok_rows)[None, :]
    place = jnp.einsum(
        "set,tu->seu", named.astype(BF16), before.astype(BF16), preferred_element_type=F32
    ).astype(jnp.int32)
    slots = jnp.arange(capacity, dtype=jnp.int32)
    pick = (place[:, :, None, :] == slots[None, None, :, None]) & named[:, :, None, :]
    slot_weight = jnp.sum(jnp.where(pick, weight[:, :, None, :], 0.0), axis=3)
    return pick.astype(BF16), slot_weight


def per_device(soft_tokens, expert_ids, gate_mix, w_gate, w_up, w_down, out_grad):
    tok_rows, width_part = soft_tokens.shape
    top_count = expert_ids.shape[1]
    local_experts = w_gate.shape[0]
    hidden = w_gate.shape[2]
    groups = lax.axis_size("expert")
    dp_count = lax.axis_size("dp")
    experts = groups * local_experts
    capacity = max(2, tok_rows * top_count * 5 // (4 * experts))
    both = lax.all_gather(jnp.concatenate([soft_tokens, out_grad], axis=1), "expert")
    ids = lax.all_gather(expert_ids, "expert")
    mix = lax.all_gather(gate_mix, "expert")
    first = lax.axis_index("expert") * local_experts
    pick, slot_weight = slot_maps(ids, mix, first, local_experts, capacity)
    rows = jnp.einsum("sect,std->secd", pick, both, preferred_element_type=F32).astype(BF16)
    pre = [
        jnp.einsum("secd,edf->secf", rows[..., :width_part], w, preferred_element_type=F32)
        for w in (w_gate, w_up)
    ]
    back = jnp.einsum("secd,efd->secf", rows[..., width_part:], w_down, preferred_element_type=F32)
    part = jnp.concatenate(pre + [back], axis=-1).astype(BF16)
    total = part.astype(F32)
    moved = part
    for _ in range(dp_count - 1):
        moved = lax.ppermute(moved, "dp", [(i, (i + 1) % dp_count) for i in range(dp_count)])
        total = total + moved.astype(F32)
    a = total[..., :hidden]
    b = total[..., hidden : 2 * hidden]
    back = total[..., 2 * hidden :] * slot_weight[..., None]
    sig = jax.nn.sigmoid(a)
    act = (a * sig * b * slot_weight[..., None]).astype(BF16)
    d_gate = (back * b * sig * (1.0 + a * (1.0 - sig))).astype(BF16)
    d_up = (back * a * sig).astype(BF16)
    out = jnp.einsum("secf,efd->secd", act, w_down, preferred_element_type=F32)
    grad = jnp.einsum("secf,edf->secd", d_gate, w_gate, preferred_element_type=F32) + jnp.einsum(
        "secf,edf->secd", d_up, w_up, preferred_element_type=F32
    )
    result = jnp.concatenate([out, grad], axis=-1).astype(BF16)
    spread = jnp.einsum("sect,secd->std", pick, result, preferred_element_type=F32).astype(BF16)
    summed = lax.psum_scatter(spread, "expert", scatter_dimension=0, tiled=False)
    return summed[:, :width_part], summed[:, width_part:]


MESH = pl.DeviceIdType.MESH
MID = 2
CORES = 2
AHEAD = 2


def flip(value, step, count):
    out, bit = 0, 1
    while bit < count:
        out = out + lax.rem(lax.div(value, bit) + lax.div(step, bit), 2) * bit
        bit *= 2
    return out


def fused_kernel(
    groups, slots, tok_ref, cot_ref, ids_ref, mix_ref, wg_hbm, wu_hbm, wd_hbm, mixed_ref, tgrad_ref,
    wg_ref, wu_ref, wd_ref, ag_tok, ag_cot, table, metas,
    ysend_pre, yrecv_pre, ysend_back, yrecv_back, acc, crecv, hold, xsend, xrecv, zsend, zrecv,
    wsem, ms, mr, zs, zr, xs, xr, cs, cr, ys, yr, rcs, rcr, rxs, rxr, rzs, rzr,
):
    rows, half = tok_ref.shape
    experts, _, hid = wg_ref.shape
    plane = MID * CORES
    outer = groups // plane
    units = 2 * outer
    me = lax.axis_index("expert")
    y = lax.axis_index("dp")
    z = lax.div(me, plane)
    x = lax.rem(lax.div(me, CORES), MID)
    c = lax.rem(me, CORES)
    core_peer = (z * MID + x) * CORES + 1 - c
    x_peer = (z * MID + 1 - x) * CORES + c
    other_dp = {"dp": 1 - y, "expert": me}
    ag = (ag_tok, ag_cot)
    own = (tok_ref, cot_ref)
    ysend, yrecv = (ysend_pre, ysend_back), (yrecv_pre, yrecv_back)

    def at(expert):
        return {"dp": y, "expert": expert}

    def copy(src, dst, send, recv, device):
        return pltpu.make_async_remote_copy(
            src_ref=src, dst_ref=dst, send_sem=send, recv_sem=recv,
            device_id=device, device_id_type=MESH,
        )

    barrier = pltpu.get_barrier_semaphore()
    for k in range(1, groups):
        pl.semaphore_signal(
            barrier, inc=1, device_id=at(lax.rem(me + k, groups)), device_id_type=MESH
        )
    pl.semaphore_signal(barrier, inc=1, device_id=other_dp, device_id_type=MESH)

    loads = [
        pltpu.make_async_copy(src, dst, wsem.at[k])
        for k, (src, dst) in enumerate(((wg_hbm, wg_ref), (wu_hbm, wu_ref), (wd_hbm, wd_ref)))
    ]
    for load in loads:
        load.start()

    def dot(a, b, dims):
        return lax.dot_general(a, b, (dims, ((), ())), preferred_element_type=F32)

    def make_table():
        total = groups * experts
        expert = lax.broadcasted_iota(jnp.int32, (total, rows), 0)
        named = jnp.zeros((total, rows), F32)
        weight = jnp.zeros((total, rows), F32)
        for k in range(ids_ref.shape[0]):
            hit = expert == ids_ref[k : k + 1, :]
            named = named + jnp.where(hit, 1.0, 0.0)
            weight = weight + jnp.where(hit, mix_ref[k : k + 1, :], 0.0)
        before = lax.broadcasted_iota(jnp.int32, (rows, rows), 0) < lax.broadcasted_iota(
            jnp.int32, (rows, rows), 1
        )
        before = jnp.where(before, 1.0, 0.0).astype(BF16)
        place = dot(named.astype(BF16), before, ((1,), (0,)))
        key = jnp.where(named > 0.0, place, -4.0 * slots)
        table[...] = jnp.zeros_like(table)
        for d in range(groups):
            span = slice(d * experts, (d + 1) * experts)
            table[d, :experts, :] = key[span]
            table[d, experts : 2 * experts, :] = weight[span]

    make_table()
    ag_tok[me] = tok_ref[...]
    ag_cot[me] = cot_ref[...]
    metas[me] = table[me]
    pl.semaphore_wait(barrier, groups)

    def meta_copy(to):
        return copy(table.at[to], metas.at[me], ms.at[to], mr.at[me], at(to))

    def meta_arrival(source):
        return copy(table.at[source], metas.at[source], ms.at[source], mr.at[source], at(source))

    def peer_of(step):
        return (flip(z, step, outer) * MID + x) * CORES + c

    def z_copy(step, part):
        return copy(own[part], ag[part].at[me], zs.at[step, part], zr.at[step, part], at(peer_of(step)))

    def z_arrival(step, part):
        blk = peer_of(step)
        return copy(own[part], ag[part].at[blk], zs.at[step, part], zr.at[step, part], at(blk))

    def x_copy(step, part, blk):
        return copy(
            ag[part].at[blk], ag[part].at[blk], xs.at[step, part], xr.at[step, part], at(x_peer)
        )

    def c_copy(step, across, part, blk):
        return copy(
            ag[part].at[blk], ag[part].at[blk],
            cs.at[step, across, part], cr.at[step, across, part], at(core_peer),
        )

    def y_copy(u, part):
        return copy(ysend[part].at[u], yrecv[part].at[u], ys.at[u, part], yr.at[u, part], other_dp)

    def rc_copy(u, part):
        return copy(
            acc.at[part, 1 - c], crecv.at[u, part], rcs.at[u, part], rcr.at[u, part], at(core_peer)
        )

    def rx_copy(step, part):
        return copy(
            xsend.at[step, part], xrecv.at[step, part],
            rxs.at[step, part], rxr.at[step, part], at(x_peer),
        )

    def rz_copy(step, part):
        return copy(
            zsend.at[step, part], zrecv.at[step, part],
            rzs.at[step, part], rzr.at[step, part], at(peer_of(step)),
        )

    def step_of(u):
        g = lax.rem(lax.div(u + 1, 2), outer)
        return (lax.rem(g, outer - 1) + 1) * lax.div(g + outer - 1, outer)

    def across_of(u):
        first = 1 - lax.div(u + units - 1, units)
        last = lax.div(u + 1, units)
        return lax.rem(u + 1, 2) + last - first

    def base_of(u):
        across = across_of(u)
        return (flip(z, step_of(u), outer) * MID + x + across - 2 * x * across) * CORES

    order = [step for step in range(2, outer)] + [1]

    for part in range(2):
        c_copy(0, 0, part, me).start()
    meta_copy(core_peer).start()
    for part in range(2):
        z_copy(order[0], part).start()
    for part in range(2):
        x_copy(0, part, me).start()

    @pl.loop(1, groups)
    def _(k):
        to = lax.rem(me + k, groups)

        @pl.when(to != core_peer)
        def _():
            meta_copy(to).start()

    for part in range(2):
        for step in order[-1:] if outer > 2 else []:
            z_copy(step, part).start()

    def pick_of(u):
        base = base_of(u)
        tiles = metas[pl.ds(base, CORES)]
        slot = lax.broadcasted_iota(jnp.int32, (CORES * slots, CORES * rows), 0).astype(F32)
        picks, weights = [], []
        for e in range(experts):
            line = jnp.concatenate(
                [tiles[b, e : e + 1] + float(b * slots) for b in range(CORES)], axis=1
            )
            share = jnp.concatenate(
                [tiles[b, experts + e : experts + e + 1] for b in range(CORES)], axis=1
            )
            match = slot == line
            picks.append(jnp.where(match, 1.0, 0.0))
            weights.append(jnp.sum(jnp.where(match, share, 0.0), axis=1, keepdims=True))
        return jnp.concatenate(picks, axis=0), weights

    lines = CORES * slots

    def first_half(u):
        step, across, base = step_of(u), across_of(u), base_of(u)
        col = base + c

        def arrive(part):
            @pl.when(across > 0)
            def _():
                x_copy(step, part, col).wait_recv()
                c_copy(step, 1, part, col).start()

            @pl.when((1 - across) * step > 0)
            def _():
                z_arrival(step, part).wait_recv()
                x_copy(step, part, col).start()
                c_copy(step, 0, part, col).start()

            c_copy(step, across, part, base + 1 - c).wait_recv()

        arrive(0)

        @pl.when(u == 0)
        def _():
            meta_arrival(core_peer).wait_recv()

        @pl.when(u == 1)
        def _():
            @pl.loop(1, groups)
            def _(k):
                source = lax.rem(me + k, groups)

                @pl.when(source != core_peer)
                def _():
                    meta_arrival(source).wait_recv()

        pick, _ = pick_of(u)
        pick = pick.astype(BF16)

        def rows_of(part):
            block = ag[part][pl.ds(base, CORES)].reshape(CORES * rows, half)
            return dot(pick, block, ((1,), (0,))).astype(BF16)

        got = rows_of(0)

        @pl.when(u == 0)
        def _():
            loads[0].wait()
            loads[1].wait()

        for e in range(experts):
            mine = got[e * lines : (e + 1) * lines]
            ysend_pre[u, e, :, :hid] = dot(mine, wg_ref[e], ((1,), (0,))).astype(BF16)
            ysend_pre[u, e, :, hid:] = dot(mine, wu_ref[e], ((1,), (0,))).astype(BF16)
        y_copy(u, 0).start()
        arrive(1)
        got = rows_of(1)

        @pl.when(u == 0)
        def _():
            loads[2].wait()

        for e in range(experts):
            mine = got[e * lines : (e + 1) * lines]
            ysend_back[u, e] = dot(mine, wd_ref[e], ((1,), (1,))).astype(BF16)

        @pl.when(u > 0)
        def _():
            y_copy(u, 1).start()

        @pl.when(u == units - 1)
        def _():
            y_copy(0, 1).start()

        for i, step_now in enumerate(order[1:-1]):
            @pl.when(u == 2 * i + 1)
            def _():
                for part in range(2):
                    z_copy(step_now, part).start()

    def sums(u, e):
        def total(lo):
            piece = ysend_pre[u, e, :, lo : lo + hid].astype(F32)
            return piece + yrecv_pre[u, e, :, lo : lo + hid].astype(F32)

        return total(0), total(hid)

    def scatter(u, part, pick, values):
        spread = dot(pick.T.astype(BF16), jnp.concatenate(values, axis=0), ((1,), (0,)))
        acc[part] = spread.astype(BF16).reshape(CORES, rows, half)
        rc_copy(u, part).start()

    def mixed_half(u):
        pick, weights = pick_of(u)
        y_copy(u, 0).wait_recv()
        outs = []
        for e in range(experts):
            a, b = sums(u, e)
            act = (a * jax.nn.sigmoid(a) * b * weights[e]).astype(BF16)
            outs.append(dot(act, wd_ref[e], ((1,), (0,))).astype(BF16))
        scatter(u, 0, pick, outs)

    def grad_half(u):
        pick, weights = pick_of(u)
        y_copy(u, 1).wait_recv()
        grads = []
        for e in range(experts):
            a, b = sums(u, e)
            back = ysend_back[u, e].astype(F32) + yrecv_back[u, e].astype(F32)
            back = back * weights[e]
            sig = jax.nn.sigmoid(a)
            d_gate = (back * b * sig * (1.0 + a * (1.0 - sig))).astype(BF16)
            d_up = (back * a * sig).astype(BF16)
            grads.append(
                (dot(d_gate, wg_ref[e], ((1,), (1,))) + dot(d_up, wu_ref[e], ((1,), (1,)))).astype(BF16)
            )
        scatter(u, 1, pick, grads)

    def to_x_peer(u, part):
        step, across = step_of(u), across_of(u)
        rc_copy(u, part).wait_recv()
        both = (acc[part, c].astype(F32) + crecv[u, part].astype(F32)).astype(BF16)

        @pl.when(across == 0)
        def _():
            hold[step, part] = both

        @pl.when(across > 0)
        def _():
            xsend[step, part] = both
            rx_copy(step, part).start()

        rc_copy(u, part).wait_send()

    def to_owner(step, part):
        rx_copy(step, part).wait_recv()
        here = hold[step, part].astype(F32) + xrecv[step, part].astype(F32)
        zsend[step, part] = here.astype(BF16)
        rz_copy(step, part).start()

    @pl.loop(0, units + AHEAD)
    def _(i):
        @pl.when(i < units)
        def _():
            first_half(i)

        @pl.when(i >= AHEAD)
        def _():
            u = i - AHEAD

            @pl.when((u > 1) & (lax.rem(u, 2) == 1))
            def _():
                for part in range(2):
                    to_owner(step_of(u - 1), part)

            mixed_half(u)
            to_x_peer(u, 0)

            @pl.when(u > 0)
            def _():
                grad_half(u)
                to_x_peer(u, 1)

    def finish(part, out_ref):
        rx_copy(0, part).wait_recv()
        final = hold[0, part].astype(F32) + xrecv[0, part].astype(F32)
        for step in order:
            rz_copy(step, part).wait_recv()
            final = final + zrecv[step, part].astype(F32)
        out_ref[...] = final.astype(BF16)

    finish(0, mixed_ref)
    grad_half(0)
    to_x_peer(0, 1)
    finish(1, tgrad_ref)

    @pl.loop(1, groups)
    def _(k):
        meta_copy(lax.rem(me + k, groups)).wait_send()

    for part in range(2):
        for step in range(outer):
            x_copy(step, part, me).wait_send()
            rx_copy(step, part).wait_send()
            for across in range(2):
                c_copy(step, across, part, me).wait_send()
            if step:
                z_copy(step, part).wait_send()
                rz_copy(step, part).wait_send()
        for u in range(units):
            y_copy(u, part).wait_send()


def fused_device(soft_tokens, expert_ids, gate_mix, w_gate, w_up, w_down, out_grad):
    tok_rows, width_part = soft_tokens.shape
    top_count = expert_ids.shape[1]
    local_experts, _, hid = w_gate.shape
    groups = lax.axis_size("expert")
    experts = groups * local_experts
    capacity = max(2, tok_rows * top_count * 5 // (4 * experts))
    plane = MID * CORES
    outer = groups // plane
    units = 2 * outer
    lines = CORES * capacity
    vmem = pl.BlockSpec(memory_space=pltpu.VMEM)
    hbm = pl.BlockSpec(memory_space=pl.ANY)
    dma = pltpu.SemaphoreType.DMA
    out = jax.ShapeDtypeStruct((tok_rows, width_part), BF16)
    table_rows = -(-2 * local_experts // 8) * 8
    block = (tok_rows, width_part)
    return pl.pallas_call(
        functools.partial(fused_kernel, groups, capacity),
        out_shape=(out, out),
        in_specs=[vmem] * 4 + [hbm] * 3,
        out_specs=(vmem, vmem),
        scratch_shapes=[
            pltpu.VMEM(w_gate.shape, BF16),
            pltpu.VMEM(w_up.shape, BF16),
            pltpu.VMEM(w_down.shape, BF16),
            pltpu.VMEM((groups, *block), BF16),
            pltpu.VMEM((groups, *block), BF16),
            pltpu.VMEM((groups, table_rows, tok_rows), F32),
            pltpu.VMEM((groups, table_rows, tok_rows), F32),
            pltpu.VMEM((units, local_experts, lines, 2 * hid), BF16),
            pltpu.VMEM((units, local_experts, lines, 2 * hid), BF16),
            pltpu.VMEM((units, local_experts, lines, hid), BF16),
            pltpu.VMEM((units, local_experts, lines, hid), BF16),
            pltpu.VMEM((2, CORES, *block), BF16),
            pltpu.VMEM((units, 2, *block), BF16),
            pltpu.VMEM((outer, 2, *block), BF16),
            pltpu.VMEM((outer, 2, *block), BF16),
            pltpu.VMEM((outer, 2, *block), BF16),
            pltpu.VMEM((outer, 2, *block), BF16),
            pltpu.VMEM((outer, 2, *block), BF16),
            dma((3,)),
            dma((groups,)), dma((groups,)),
            dma((outer, 2)), dma((outer, 2)),
            dma((outer, 2)), dma((outer, 2)),
            dma((outer, 2, 2)), dma((outer, 2, 2)),
            dma((units, 2)), dma((units, 2)),
            dma((units, 2)), dma((units, 2)),
            dma((outer, 2)), dma((outer, 2)),
            dma((outer, 2)), dma((outer, 2)),
        ],
        compiler_params=pltpu.CompilerParams(
            collective_id=0, has_side_effects=True, vmem_limit_bytes=67043328
        ),
    )(soft_tokens, out_grad, expert_ids.T, gate_mix.T, w_gate, w_up, w_down)


def solution(mesh):
    in_specs = (
        P("expert", "dp"),
        P("expert", None),
        P("expert", None),
        P("expert", "dp", None),
        P("expert", "dp", None),
        P("expert", None, "dp"),
        P("expert", "dp"),
    )
    out_specs = (P("expert", "dp"), P("expert", "dp"))
    fits = mesh.shape["dp"] == 2 and mesh.shape["expert"] in (8, 16)
    return jax.shard_map(
        fused_device if fits else per_device,
        mesh=mesh, in_specs=in_specs, out_specs=out_specs, check_vma=False,
    )
```

time: 202 us -> 165 us (0.82)
  Pallas kernels: 193 us -> 161 us
  other arithmetic: 4 us -> 0 us
    pallas_call x1, Pallas kernels: 193 us -> 161 us  [fused_device(): pl.pallas_call(functools.partial(fused_kernel, groups, capacity), out_sha...]
    concatenate x2 -> x0, other arithmetic: 2.51 us -> none  [the longest x1 1.86 us: fused_device(): both = jnp.concatenate([soft_tokens, out_grad], axis=1)]
where the time goes in v1:
time: 165 us
  Pallas kernels  161 us (98%)
  local copies, waits for them, and re-layouts  3.34 us (2%)
    pallas_call x1, Pallas kernels, fused_device(): pl.pallas_call(functools.partial(fused_kernel, groups, capacity), out_sha...  161 us
    unnamed x2, local copies, waits for them, and re-layouts  3.34 us

profile of v1, /device:TPU:0, one launch (start us, length us, event | category | flops | bytes accessed | tf_op | source)
XLA Modules:
  0.0 164.7 jit_solution(15323615809950082309)
XLA Ops:
  0.6 160.7 %shard_map.86 = (bf16[128,1024]{1,0:T(8,128)(2,1)}, bf16[128,1024]{1,0:T(8,128)(2,1)}) custom-call(bf16[128,1024]{1,0:T(8,128)(2,1)} %tok_ref.1, bf16[128,1024]{1,0:T(8,128)(2,1)} %cot_ref.1, s32[8,128]{1,0:T(8,128)} %bitcast.2, f32[8,128]{1,0:T(8,128)} %bitcast.3, bf16[2,1024,768]{2,1,0:T(8,128)(2,1)} %wg_hbm.1, bf16[2,1024,768]{2,1,0:T(8,128)(2,1)} %wu_hbm.1, ...), custom_call_target="tpu_custom_call" | custom-call | tf_op jit(solution)/shard_map/pallas_call | solution.py:472
  161.3 1.7 %copy.11 = bf16[128,1024]{1,0:T(8,128)(2,1)} copy(bf16[128,1024]{1,0:T(8,128)(2,1)} %get-tuple-element.4) | data formatting | bytes 524288
  163.0 1.7 %copy.12 = bf16[128,1024]{1,0:T(8,128)(2,1)} copy(bf16[128,1024]{1,0:T(8,128)(2,1)} %get-tuple-element.5) | data formatting | bytes 524288

commit v2 on v1

--- a/solution.py
+++ b/solution.py
@@ -73,7 +73,12 @@
 MESH = pl.DeviceIdType.MESH
 MID = 2
 CORES = 2
-AHEAD = 2
+AHEAD = 4
+
+
+def same(a, b):
+    gap = (a - b) * (a - b)
+    return 1 - lax.div(2 * gap, gap + 1)
 
 
 def flip(value, step, count):
@@ -85,12 +90,12 @@
 
 
 def fused_kernel(
-    groups, slots, tok_ref, cot_ref, ids_ref, mix_ref, wg_hbm, wu_hbm, wd_hbm, mixed_ref, tgrad_ref,
-    wg_ref, wu_ref, wd_ref, ag_tok, ag_cot, table, metas,
-    ysend_pre, yrecv_pre, ysend_back, yrecv_back, acc, crecv, hold, xsend, xrecv, zsend, zrecv,
-    wsem, ms, mr, zs, zr, xs, xr, cs, cr, ys, yr, rcs, rcr, rxs, rxr, rzs, rzr,
+    groups, slots, tok_hbm, cot_hbm, ids_hbm, mix_hbm, wg_hbm, wu_hbm, wd_hbm, mixed_hbm, tgrad_hbm,
+    ids_ref, mix_ref, wg_ref, wu_ref, wd_ref, ag_tok, ag_cot, table, metas,
+    ysend_pre, yrecv_pre, ysend_back, yrecv_back, ready, acc, crecv, hold, xsend, xrecv, zsend, zrecv,
+    lsem, wsem, osem, ms, mr, zs, zr, xs, xr, cs, cr, ys, yr, rcs, rcr, rxs, rxr, rzs, rzr,
 ):
-    rows, half = tok_ref.shape
+    rows, half = tok_hbm.shape
     experts, _, hid = wg_ref.shape
     plane = MID * CORES
     outer = groups // plane
@@ -104,7 +109,7 @@
     x_peer = (z * MID + 1 - x) * CORES + c
     other_dp = {"dp": 1 - y, "expert": me}
     ag = (ag_tok, ag_cot)
-    own = (tok_ref, cot_ref)
+    outputs = (mixed_hbm, tgrad_hbm)
     ysend, yrecv = (ysend_pre, ysend_back), (yrecv_pre, yrecv_back)
 
     def at(expert):
@@ -124,11 +129,21 @@
     pl.semaphore_signal(barrier, inc=1, device_id=other_dp, device_id_type=MESH)
 
     loads = [
-        pltpu.make_async_copy(src, dst, wsem.at[k])
-        for k, (src, dst) in enumerate(((wg_hbm, wg_ref), (wu_hbm, wu_ref), (wd_hbm, wd_ref)))
+        pltpu.make_async_copy(src, dst, lsem.at[k])
+        for k, (src, dst) in enumerate(
+            ((ids_hbm, ids_ref), (mix_hbm, mix_ref), (tok_hbm, ag_tok.at[me]), (cot_hbm, ag_cot.at[me]))
+        )
     ]
+
+    def weight(which, e):
+        src, dst = ((wg_hbm, wg_ref), (wu_hbm, wu_ref), (wd_hbm, wd_ref))[which]
+        return pltpu.make_async_copy(src.at[e], dst.at[e], wsem.at[which, e])
+
     for load in loads:
         load.start()
+    for e in range(experts):
+        for which in range(3):
+            weight(which, e).start()
 
     def dot(a, b, dims):
         return lax.dot_general(a, b, (dims, ((), ())), preferred_element_type=F32)
@@ -154,10 +169,12 @@
             table[d, :experts, :] = key[span]
             table[d, experts : 2 * experts, :] = weight[span]
 
+    loads[0].wait()
+    loads[1].wait()
     make_table()
-    ag_tok[me] = tok_ref[...]
-    ag_cot[me] = cot_ref[...]
     metas[me] = table[me]
+    loads[2].wait()
+    loads[3].wait()
     pl.semaphore_wait(barrier, groups)
 
     def meta_copy(to):
@@ -170,11 +187,11 @@
         return (flip(z, step, outer) * MID + x) * CORES + c
 
     def z_copy(step, part):
-        return copy(own[part], ag[part].at[me], zs.at[step, part], zr.at[step, part], at(peer_of(step)))
+        return copy(ag[part].at[me], ag[part].at[me], zs.at[step, part], zr.at[step, part], at(peer_of(step)))
 
     def z_arrival(step, part):
         blk = peer_of(step)
-        return copy(own[part], ag[part].at[blk], zs.at[step, part], zr.at[step, part], at(blk))
+        return copy(ag[part].at[blk], ag[part].at[blk], zs.at[step, part], zr.at[step, part], at(blk))
 
     def x_copy(step, part, blk):
         return copy(
@@ -187,8 +204,10 @@
             cs.at[step, across, part], cr.at[step, across, part], at(core_peer),
         )
 
-    def y_copy(u, part):
-        return copy(ysend[part].at[u], yrecv[part].at[u], ys.at[u, part], yr.at[u, part], other_dp)
+    def y_copy(u, part, e):
+        return copy(
+            ysend[part].at[u, e], yrecv[part].at[u, e], ys.at[u, part, e], yr.at[u, part, e], other_dp
+        )
 
     def rc_copy(u, part):
         return copy(
@@ -214,7 +233,9 @@
     def across_of(u):
         first = 1 - lax.div(u + units - 1, units)
         last = lax.div(u + 1, units)
-        return lax.rem(u + 1, 2) + last - first
+        swap = lax.div(u + 3, units) - lax.div(u + 1, units)
+        flat = lax.rem(u + 1, 2)
+        return flat + swap * (1 - 2 * flat) + last - first
 
     def base_of(u):
         across = across_of(u)
@@ -225,18 +246,18 @@
     for part in range(2):
         c_copy(0, 0, part, me).start()
     meta_copy(core_peer).start()
+    @pl.loop(1, groups)
+    def _(k):
+        to = lax.rem(me + k, groups)
+
+        @pl.when(to != core_peer)
+        def _():
+            meta_copy(to).start()
+
     for part in range(2):
         z_copy(order[0], part).start()
     for part in range(2):
         x_copy(0, part, me).start()
-
-    @pl.loop(1, groups)
-    def _(k):
-        to = lax.rem(me + k, groups)
-
-        @pl.when(to != core_peer)
-        def _():
-            meta_copy(to).start()
 
     for part in range(2):
         for step in order[-1:] if outer > 2 else []:
@@ -261,32 +282,47 @@
 
     lines = CORES * slots
 
-    def first_half(u):
+    def hand_on(step, part, col):
+        z_arrival(step, part).wait_recv()
+        x_copy(step, part, col).start()
+        c_copy(step, 0, part, col).start()
+
+    def first_half(i, u, part):
         step, across, base = step_of(u), across_of(u), base_of(u)
         col = base + c
 
-        def arrive(part):
+        def arrive():
             @pl.when(across > 0)
             def _():
                 x_copy(step, part, col).wait_recv()
                 c_copy(step, 1, part, col).start()
 
-            @pl.when((1 - across) * step > 0)
+            @pl.when(((1 - across) * step > 0) & (u != units - 2))
             def _():
-                z_arrival(step, part).wait_recv()
-                x_copy(step, part, col).start()
-                c_copy(step, 0, part, col).start()
+                hand_on(step, part, col)
 
             c_copy(step, across, part, base + 1 - c).wait_recv()
 
-        arrive(0)
-
-        @pl.when(u == 0)
+        @pl.when(i < 2 * units)
+        def _():
+            arrive()
+
+        @pl.when(i == 0)
         def _():
             meta_arrival(core_peer).wait_recv()
-
-        @pl.when(u == 1)
-        def _():
+            weight(0, 0).wait()
+            weight(1, 0).wait()
+
+        @pl.when(i == 1)
+        def _():
+            weight(2, 0).wait()
+
+        @pl.when(i == 2)
+        def _():
+            for e in range(1, experts):
+                for which in range(3):
+                    weight(which, e).wait()
+
             @pl.loop(1, groups)
             def _(k):
                 source = lax.rem(me + k, groups)
@@ -296,48 +332,18 @@
                     meta_arrival(source).wait_recv()
 
         pick, _ = pick_of(u)
-        pick = pick.astype(BF16)
-
-        def rows_of(part):
-            block = ag[part][pl.ds(base, CORES)].reshape(CORES * rows, half)
-            return dot(pick, block, ((1,), (0,))).astype(BF16)
-
-        got = rows_of(0)
-
-        @pl.when(u == 0)
-        def _():
-            loads[0].wait()
-            loads[1].wait()
-
+        block = ag[part][pl.ds(base, CORES)].reshape(CORES * rows, half)
+        got = dot(pick.astype(BF16), block, ((1,), (0,))).astype(BF16)
         for e in range(experts):
-            mine = got[e * lines : (e + 1) * lines]
-            ysend_pre[u, e, :, :hid] = dot(mine, wg_ref[e], ((1,), (0,))).astype(BF16)
-            ysend_pre[u, e, :, hid:] = dot(mine, wu_ref[e], ((1,), (0,))).astype(BF16)
-        y_copy(u, 0).start()
-        arrive(1)
-        got = rows_of(1)
-
-        @pl.when(u == 0)
-        def _():
-            loads[2].wait()
-
-        for e in range(experts):
-            mine = got[e * lines : (e + 1) * lines]
-            ysend_back[u, e] = dot(mine, wd_ref[e], ((1,), (1,))).astype(BF16)
-
-        @pl.when(u > 0)
-        def _():
-            y_copy(u, 1).start()
-
-        @pl.when(u == units - 1)
-        def _():
-            y_copy(0, 1).start()
-
-        for i, step_now in enumerate(order[1:-1]):
-            @pl.when(u == 2 * i + 1)
+            @pl.when((i < 2 * units) if e == 0 else (i >= 2))
             def _():
-                for part in range(2):
-                    z_copy(step_now, part).start()
+                mine = got[e * lines : (e + 1) * lines]
+                if part == 0:
+                    ysend_pre[u, e, :, :hid] = dot(mine, wg_ref[e], ((1,), (0,))).astype(BF16)
+                    ysend_pre[u, e, :, hid:] = dot(mine, wu_ref[e], ((1,), (0,))).astype(BF16)
+                else:
+                    ysend_back[u, e] = dot(mine, wd_ref[e], ((1,), (1,))).astype(BF16)
+                y_copy(u, part, e).start()
 
     def sums(u, e):
         def total(lo):
@@ -346,36 +352,19 @@
 
         return total(0), total(hid)
 
-    def scatter(u, part, pick, values):
-        spread = dot(pick.T.astype(BF16), jnp.concatenate(values, axis=0), ((1,), (0,)))
-        acc[part] = spread.astype(BF16).reshape(CORES, rows, half)
-        rc_copy(u, part).start()
-
-    def mixed_half(u):
-        pick, weights = pick_of(u)
-        y_copy(u, 0).wait_recv()
-        outs = []
-        for e in range(experts):
-            a, b = sums(u, e)
-            act = (a * jax.nn.sigmoid(a) * b * weights[e]).astype(BF16)
-            outs.append(dot(act, wd_ref[e], ((1,), (0,))).astype(BF16))
-        scatter(u, 0, pick, outs)
-
-    def grad_half(u):
-        pick, weights = pick_of(u)
-        y_copy(u, 1).wait_recv()
-        grads = []
-        for e in range(experts):
-            a, b = sums(u, e)
-            back = ysend_back[u, e].astype(F32) + yrecv_back[u, e].astype(F32)
-            back = back * weights[e]
-            sig = jax.nn.sigmoid(a)
-            d_gate = (back * b * sig * (1.0 + a * (1.0 - sig))).astype(BF16)
-            d_up = (back * a * sig).astype(BF16)
-            grads.append(
-                (dot(d_gate, wg_ref[e], ((1,), (1,))) + dot(d_up, wu_ref[e], ((1,), (1,)))).astype(BF16)
-            )
-        scatter(u, 1, pick, grads)
+    def mixed_half(u, e, share):
+        a, b = sums(u, e)
+        act = (a * jax.nn.sigmoid(a) * b * share).astype(BF16)
+        return dot(act, wd_ref[e], ((1,), (0,))).astype(BF16)
+
+    def grad_half(u, e, share):
+        a, b = sums(u, e)
+        back = (ysend_back[u, e].astype(F32) + yrecv_back[u, e].astype(F32)) * share
+        sig = jax.nn.sigmoid(a)
+        d_gate = (back * b * sig * (1.0 + a * (1.0 - sig))).astype(BF16)
+        d_up = (back * a * sig).astype(BF16)
+        grad = dot(d_gate, wg_ref[e], ((1,), (1,))) + dot(d_up, wu_ref[e], ((1,), (1,)))
+        return grad.astype(BF16)
 
     def to_x_peer(u, part):
         step, across = step_of(u), across_of(u)
@@ -399,41 +388,89 @@
         zsend[step, part] = here.astype(BF16)
         rz_copy(step, part).start()
 
-    @pl.loop(0, units + AHEAD)
-    def _(i):
-        @pl.when(i < units)
-        def _():
-            first_half(i)
-
-        @pl.when(i >= AHEAD)
-        def _():
-            u = i - AHEAD
-
-            @pl.when((u > 1) & (lax.rem(u, 2) == 1))
+    def item(i):
+        first, second, third = same(i, 0), same(i, 1), same(i, 2)
+        ends = [same(i, 2 * units + k) for k in (-1, 0, 1)]
+        u = lax.div(i + 1, 2) - 1 + first + (units - 1) * (third - ends[1]) - units * ends[2]
+        part = lax.rem(i + 1, 2) - first + second - third + ends[0] - ends[1] + ends[2]
+        return u, part
+
+    def second_half(i, u, part):
+        step, before = step_of(u), step_of(u - 1 + lax.div(units - u, units))
+        kept = lax.div(units - u, units)
+
+        @pl.when((u > 1) & (u < units - 1) & (lax.rem(u, 2) == 1))
+        def _():
+            to_owner(before, part)
+
+        pick, shares = pick_of(u)
+        for e in range(experts):
+            @pl.when((i < 2 * units) if e == 0 else (i >= 2))
             def _():
-                for part in range(2):
-                    to_owner(step_of(u - 1), part)
-
-            mixed_half(u)
-            to_x_peer(u, 0)
-
-            @pl.when(u > 0)
-            def _():
-                grad_half(u)
-                to_x_peer(u, 1)
-
-    def finish(part, out_ref):
-        rx_copy(0, part).wait_recv()
-        final = hold[0, part].astype(F32) + xrecv[0, part].astype(F32)
+                y_copy(u, part, e).wait_recv()
+                ready[kept, part, e] = (grad_half if part else mixed_half)(u, e, shares[e])
+
+        @pl.when(i >= 2)
+        def _():
+            values = ready[kept, part].reshape(experts * lines, half)
+            spread = dot(pick.T.astype(BF16), values, ((1,), (0,)))
+            acc[part] = spread.astype(BF16).reshape(CORES, rows, half)
+            rc_copy(u, part).start()
+
+        @pl.when((i >= 2) & (i < 2 * units))
+        def _():
+            to_x_peer(u, part)
+
+        @pl.when(u == units - 2)
+        def _():
+            to_owner(step, part)
+
+    def out_copy(part):
+        return pltpu.make_async_copy(zsend.at[0, part], outputs[part], osem.at[part])
+
+    def finish(part):
         for step in order:
             rz_copy(step, part).wait_recv()
+        rx_copy(0, part).wait_recv()
+        final = xrecv[0, part].astype(F32)
+        for step in order:
             final = final + zrecv[step, part].astype(F32)
-        out_ref[...] = final.astype(BF16)
-
-    finish(0, mixed_ref)
-    grad_half(0)
-    to_x_peer(0, 1)
-    finish(1, tgrad_ref)
+        rc_copy(0, part).wait_recv()
+        final = final + acc[part, c].astype(F32) + crecv[0, part].astype(F32)
+        zsend[0, part] = final.astype(BF16)
+        out_copy(part).start()
+
+    @pl.loop(0, 2 * units + 2 + AHEAD)
+    def _(i):
+        @pl.when(i < 2 * units + 2)
+        def _():
+            u, part = item(i)
+            for which in range(2):
+                @pl.when(part == which)
+                def _():
+                    first_half(i, u, which)
+
+            @pl.when(i == 2 * outer - 2)
+            def _():
+                for which in range(2):
+                    hand_on(order[-1], which, peer_of(order[-1]))
+
+            for later, step in enumerate(order[1:-1]):
+                @pl.when(i == 4 * later + 4)
+                def _():
+                    for which in range(2):
+                        z_copy(step, which).start()
+
+        @pl.when(i >= AHEAD)
+        def _():
+            u, part = item(i - AHEAD)
+            for which in range(2):
+                @pl.when(part == which)
+                def _():
+                    second_half(i - AHEAD, u, which)
+
+    finish(0)
+    finish(1)
 
     @pl.loop(1, groups)
     def _(k):
@@ -449,7 +486,22 @@
                 z_copy(step, part).wait_send()
                 rz_copy(step, part).wait_send()
         for u in range(units):
-            y_copy(u, part).wait_send()
+            for e in range(experts):
+                y_copy(u, part, e).wait_send()
+        rc_copy(0, part).wait_send()
+        out_copy(part).wait()
+
+
+def deliver(*parts):
+    def move(a_ref, b_ref, c_ref, d_ref):
+        c_ref[...] = a_ref[...]
+        d_ref[...] = b_ref[...]
+
+    spec = pl.BlockSpec(memory_space=pltpu.VMEM)
+    return pl.pallas_call(
+        move, out_shape=tuple(jax.ShapeDtypeStruct(p.shape, p.dtype) for p in parts),
+        in_specs=[spec, spec], out_specs=(spec, spec),
+    )(*parts)
 
 
 def fused_device(soft_tokens, expert_ids, gate_mix, w_gate, w_up, w_down, out_grad):
@@ -463,18 +515,19 @@
     outer = groups // plane
     units = 2 * outer
     lines = CORES * capacity
-    vmem = pl.BlockSpec(memory_space=pltpu.VMEM)
     hbm = pl.BlockSpec(memory_space=pl.ANY)
     dma = pltpu.SemaphoreType.DMA
     out = jax.ShapeDtypeStruct((tok_rows, width_part), BF16)
     table_rows = -(-2 * local_experts // 8) * 8
     block = (tok_rows, width_part)
-    return pl.pallas_call(
+    parts = pl.pallas_call(
         functools.partial(fused_kernel, groups, capacity),
         out_shape=(out, out),
-        in_specs=[vmem] * 4 + [hbm] * 3,
-        out_specs=(vmem, vmem),
+        in_specs=[hbm] * 7,
+        out_specs=(hbm, hbm),
         scratch_shapes=[
+            pltpu.VMEM((top_count, tok_rows), jnp.int32),
+            pltpu.VMEM((top_count, tok_rows), F32),
             pltpu.VMEM(w_gate.shape, BF16),
             pltpu.VMEM(w_up.shape, BF16),
             pltpu.VMEM(w_down.shape, BF16),
@@ -486,6 +539,7 @@
             pltpu.VMEM((units, local_experts, lines, 2 * hid), BF16),
             pltpu.VMEM((units, local_experts, lines, hid), BF16),
             pltpu.VMEM((units, local_experts, lines, hid), BF16),
+            pltpu.VMEM((2, 2, local_experts, lines, width_part), BF16),
             pltpu.VMEM((2, CORES, *block), BF16),
             pltpu.VMEM((units, 2, *block), BF16),
             pltpu.VMEM((outer, 2, *block), BF16),
@@ -493,12 +547,12 @@
             pltpu.VMEM((outer, 2, *block), BF16),
             pltpu.VMEM((outer, 2, *block), BF16),
             pltpu.VMEM((outer, 2, *block), BF16),
-            dma((3,)),
+            dma((4,)), dma((3, local_experts)), dma((2,)),
             dma((groups,)), dma((groups,)),
             dma((outer, 2)), dma((outer, 2)),
             dma((outer, 2)), dma((outer, 2)),
             dma((outer, 2, 2)), dma((outer, 2, 2)),
-            dma((units, 2)), dma((units, 2)),
+            dma((units, 2, local_experts)), dma((units, 2, local_experts)),
             dma((units, 2)), dma((units, 2)),
             dma((outer, 2)), dma((outer, 2)),
             dma((outer, 2)), dma((outer, 2)),
@@ -507,6 +561,7 @@
             collective_id=0, has_side_effects=True, vmem_limit_bytes=67043328
         ),
     )(soft_tokens, out_grad, expert_ids.T, gate_mix.T, w_gate, w_up, w_down)
+    return deliver(*parts)
 
 
 def solution(mesh):

time: 165 us -> 149 us (0.903)
  Pallas kernels: 161 us -> 147 us
  local copies, waits for them, and re-layouts: 3.34 us -> 0 us
    pallas_call x1, Pallas kernels: 161 us -> 145 us  [fused_device(): pl.pallas_call(functools.partial(fused_kernel, groups, capacity), out_sha...]
    unnamed x2 -> x0, local copies, waits for them, and re-layouts: 3.34 us -> none
    pallas_call x0 -> x1, Pallas kernels: none -> 1.84 us  [deliver(): pl.pallas_call(move, out_shape=tuple((jax.ShapeDtypeStruct(p.shape, p.dty...]
where the time goes in v2:
time: 149 us; the launch traced here: 147 us
  Pallas kernels  147 us (99%)
    pallas_call x1, Pallas kernels, fused_device(): pl.pallas_call(functools.partial(fused_kernel, groups, capacity), out_sha...  145 us

profile of v2, /device:TPU:0, one launch (start us, length us, event | category | flops | bytes accessed | tf_op | source)
XLA Modules:
  0.0 147.4 jit_solution(3811231939105135045)
XLA Ops:
  0.6 145.0 %shard_map.86 = (bf16[128,1024]{1,0:T(8,128)(2,1)}, bf16[128,1024]{1,0:T(8,128)(2,1)}) custom-call(bf16[128,1024]{1,0:T(8,128)(2,1)} %tok_hbm.1, bf16[128,1024]{1,0:T(8,128)(2,1)} %cot_hbm.1, s32[8,128]{1,0:T(8,128)} %bitcast.2, f32[8,128]{1,0:T(8,128)} %bitcast.3, bf16[2,1024,768]{2,1,0:T(8,128)(2,1)} %wg_hbm.1, bf16[2,1024,768]{2,1,0:T(8,128)(2,1)} %wu_hbm.1, ...), custom_call_target="tpu_custom_call" | custom-call | tf_op jit(solution)/shard_map/pallas_call | solution.py:523
  145.6 1.8 %shard_map.87 = (bf16[128,1024]{1,0:T(8,128)(2,1)}, bf16[128,1024]{1,0:T(8,128)(2,1)}) custom-call(bf16[128,1024]{1,0:T(8,128)(2,1)} %get-tuple-element.4.a_ref, bf16[128,1024]{1,0:T(8,128)(2,1)} %get-tuple-element.5.b_ref), custom_call_target="tpu_custom_call" | custom-call | tf_op jit(solution)/shard_map/pallas_call | solution.py:501

commit v3 on v2

--- a/solution.py
+++ b/solution.py
@@ -307,9 +307,14 @@
         def _():
             arrive()
 
+            if part == 0:
+                for b in range(CORES):
+                    @pl.when(base + b != me)
+                    def _():
+                        meta_arrival(base + b).wait_recv()
+
         @pl.when(i == 0)
         def _():
-            meta_arrival(core_peer).wait_recv()
             weight(0, 0).wait()
             weight(1, 0).wait()
 
@@ -322,14 +327,6 @@
             for e in range(1, experts):
                 for which in range(3):
                     weight(which, e).wait()
-
-            @pl.loop(1, groups)
-            def _(k):
-                source = lax.rem(me + k, groups)
-
-                @pl.when(source != core_peer)
-                def _():
-                    meta_arrival(source).wait_recv()
 
         pick, _ = pick_of(u)
         block = ag[part][pl.ds(base, CORES)].reshape(CORES * rows, half)
@@ -389,10 +386,9 @@
         rz_copy(step, part).start()
 
     def item(i):
-        first, second, third = same(i, 0), same(i, 1), same(i, 2)
-        ends = [same(i, 2 * units + k) for k in (-1, 0, 1)]
-        u = lax.div(i + 1, 2) - 1 + first + (units - 1) * (third - ends[1]) - units * ends[2]
-        part = lax.rem(i + 1, 2) - first + second - third + ends[0] - ends[1] + ends[2]
+        pair = lax.div(i, 2)
+        moved = (units - 1) * (same(pair, 1) - same(pair, units))
+        u, part = pair - 1 + same(pair, 0) + moved, lax.rem(i, 2)
         return u, part
 
     def second_half(i, u, part):
@@ -437,8 +433,7 @@
             final = final + zrecv[step, part].astype(F32)
         rc_copy(0, part).wait_recv()
         final = final + acc[part, c].astype(F32) + crecv[0, part].astype(F32)
-        zsend[0, part] = final.astype(BF16)
-        out_copy(part).start()
+        outputs[part][...] = final.astype(BF16)
 
     @pl.loop(0, 2 * units + 2 + AHEAD)
     def _(i):
@@ -450,13 +445,13 @@
                 def _():
                     first_half(i, u, which)
 
-            @pl.when(i == 2 * outer - 2)
+            @pl.when(i == 2 * outer - 1)
             def _():
                 for which in range(2):
                     hand_on(order[-1], which, peer_of(order[-1]))
 
             for later, step in enumerate(order[1:-1]):
-                @pl.when(i == 4 * later + 4)
+                @pl.when(i == 4 * later + 5)
                 def _():
                     for which in range(2):
                         z_copy(step, which).start()
@@ -489,19 +484,6 @@
             for e in range(experts):
                 y_copy(u, part, e).wait_send()
         rc_copy(0, part).wait_send()
-        out_copy(part).wait()
-
-
-def deliver(*parts):
-    def move(a_ref, b_ref, c_ref, d_ref):
-        c_ref[...] = a_ref[...]
-        d_ref[...] = b_ref[...]
-
-    spec = pl.BlockSpec(memory_space=pltpu.VMEM)
-    return pl.pallas_call(
-        move, out_shape=tuple(jax.ShapeDtypeStruct(p.shape, p.dtype) for p in parts),
-        in_specs=[spec, spec], out_specs=(spec, spec),
-    )(*parts)
 
 
 def fused_device(soft_tokens, expert_ids, gate_mix, w_gate, w_up, w_down, out_grad):
@@ -517,14 +499,14 @@
     lines = CORES * capacity
     hbm = pl.BlockSpec(memory_space=pl.ANY)
     dma = pltpu.SemaphoreType.DMA
-    out = jax.ShapeDtypeStruct((tok_rows, width_part), BF16)
+    out = pltpu.VMEM((tok_rows, width_part), BF16)
     table_rows = -(-2 * local_experts // 8) * 8
     block = (tok_rows, width_part)
-    parts = pl.pallas_call(
+    return pl.pallas_call(
         functools.partial(fused_kernel, groups, capacity),
         out_shape=(out, out),
         in_specs=[hbm] * 7,
-        out_specs=(hbm, hbm),
+        out_specs=(pl.BlockSpec(memory_space=pltpu.VMEM),) * 2,
         scratch_shapes=[
             pltpu.VMEM((top_count, tok_rows), jnp.int32),
             pltpu.VMEM((top_count, tok_rows), F32),
@@ -558,10 +540,9 @@
             dma((outer, 2)), dma((outer, 2)),
         ],
         compiler_params=pltpu.CompilerParams(
-            collective_id=0, has_side_effects=True, vmem_limit_bytes=67043328
+            collective_id=0, has_side_effects=True, vmem_limit_bytes=60 * 1024 * 1024
         ),
     )(soft_tokens, out_grad, expert_ids.T, gate_mix.T, w_gate, w_up, w_down)
-    return deliver(*parts)
 
 
 def solution(mesh):

time: 149 us -> 145 us (0.973); the launches traced: 147 us -> 145 us
  Pallas kernels: 147 us -> 143 us
    pallas_call x1, Pallas kernels: 145 us -> 143 us  [fused_device(): pl.pallas_call(functools.partial(fused_kernel, groups, capacity), out_sha...]
    pallas_call x1 -> x0, Pallas kernels: 1.84 us -> none  [deliver(): pl.pallas_call(move, out_shape=tuple((jax.ShapeDtypeStruct(p.shape, p.dty...]
where the time goes in v3:
time: 145 us
  Pallas kernels  143 us (99%)
    pallas_call x1, Pallas kernels, fused_device(): pl.pallas_call(functools.partial(fused_kernel, groups, capacity), out_sha...  143 us

profile of v3, /device:TPU:0, one launch (start us, length us, event | category | flops | bytes accessed | tf_op | source)
XLA Modules:
  0.0 145.1 jit_solution(16841823375087669756)
XLA Ops:
  0.6 143.0 %shard_map.86 = (bf16[128,1024]{1,0:T(8,128)(2,1)S(1)}, bf16[128,1024]{1,0:T(8,128)(2,1)S(1)}) custom-call(bf16[128,1024]{1,0:T(8,128)(2,1)} %tok_hbm.1, bf16[128,1024]{1,0:T(8,128)(2,1)} %cot_hbm.1, s32[8,128]{1,0:T(8,128)} %bitcast.2, f32[8,128]{1,0:T(8,128)} %bitcast.3, bf16[2,1024,768]{2,1,0:T(8,128)(2,1)} %wg_hbm.1, bf16[2,1024,768]{2,1,0:T(8,128)(2,1)} %wu_hbm.1, ...), custom_call_target="tpu_custom_call" | custom-call | tf_op jit(solution)/shard_map/pallas_call | solution.py:505
  143.7 0.7 copy.11
  144.4 0.7 copy.12

commit v4 on v3

--- a/solution.py
+++ b/solution.py
@@ -350,16 +350,20 @@
         return total(0), total(hid)
 
     def mixed_half(u, e, share):
+        y_copy(u, 0, e).wait_recv()
         a, b = sums(u, e)
         act = (a * jax.nn.sigmoid(a) * b * share).astype(BF16)
         return dot(act, wd_ref[e], ((1,), (0,))).astype(BF16)
 
     def grad_half(u, e, share):
         a, b = sums(u, e)
+        sig = jax.nn.sigmoid(a)
+        by_gate = b * sig * (1.0 + a * (1.0 - sig))
+        by_up = a * sig
+        y_copy(u, 1, e).wait_recv()
         back = (ysend_back[u, e].astype(F32) + yrecv_back[u, e].astype(F32)) * share
-        sig = jax.nn.sigmoid(a)
-        d_gate = (back * b * sig * (1.0 + a * (1.0 - sig))).astype(BF16)
-        d_up = (back * a * sig).astype(BF16)
+        d_gate = (back * by_gate).astype(BF16)
+        d_up = (back * by_up).astype(BF16)
         grad = dot(d_gate, wg_ref[e], ((1,), (1,))) + dot(d_up, wu_ref[e], ((1,), (1,)))
         return grad.astype(BF16)
 
@@ -400,16 +404,16 @@
             to_owner(before, part)
 
         pick, shares = pick_of(u)
+        spread_by = pick.T.astype(BF16)
         for e in range(experts):
             @pl.when((i < 2 * units) if e == 0 else (i >= 2))
             def _():
-                y_copy(u, part, e).wait_recv()
                 ready[kept, part, e] = (grad_half if part else mixed_half)(u, e, shares[e])
 
         @pl.when(i >= 2)
         def _():
             values = ready[kept, part].reshape(experts * lines, half)
-            spread = dot(pick.T.astype(BF16), values, ((1,), (0,)))
+            spread = dot(spread_by, values, ((1,), (0,)))
             acc[part] = spread.astype(BF16).reshape(CORES, rows, half)
             rc_copy(u, part).start()
 
@@ -484,6 +488,25 @@
             for e in range(experts):
                 y_copy(u, part, e).wait_send()
         rc_copy(0, part).wait_send()
+
+
+def deliver(*parts):
+    def move(a_ref, b_ref, c_ref, d_ref, sem):
+        copies = [
+            pltpu.make_async_copy(src, dst, sem.at[k])
+            for k, (src, dst) in enumerate(((a_ref, c_ref), (b_ref, d_ref)))
+        ]
+        for one in copies:
+            one.start()
+        for one in copies:
+            one.wait()
+
+    return pl.pallas_call(
+        move, out_shape=tuple(jax.ShapeDtypeStruct(p.shape, p.dtype) for p in parts),
+        in_specs=[pl.BlockSpec(memory_space=pltpu.VMEM)] * 2,
+        out_specs=(pl.BlockSpec(memory_space=pl.ANY),) * 2,
+        scratch_shapes=[pltpu.SemaphoreType.DMA((2,))],
+    )(*(pltpu.with_memory_space_constraint(p, pltpu.VMEM) for p in parts))
 
 
 def fused_device(soft_tokens, expert_ids, gate_mix, w_gate, w_up, w_down, out_grad):
@@ -502,7 +525,7 @@
     out = pltpu.VMEM((tok_rows, width_part), BF16)
     table_rows = -(-2 * local_experts // 8) * 8
     block = (tok_rows, width_part)
-    return pl.pallas_call(
+    parts = pl.pallas_call(
         functools.partial(fused_kernel, groups, capacity),
         out_shape=(out, out),
         in_specs=[hbm] * 7,
@@ -543,6 +566,7 @@
             collective_id=0, has_side_effects=True, vmem_limit_bytes=60 * 1024 * 1024
         ),
     )(soft_tokens, out_grad, expert_ids.T, gate_mix.T, w_gate, w_up, w_down)
+    return deliver(*parts)
 
 
 def solution(mesh):

time: 145 us -> 145 us (level)
  no operation moved by 1% of the time
where the time goes in v4:
time: 145 us; the launch traced here: 144 us
  Pallas kernels  144 us (99%)
    pallas_call x1, Pallas kernels, fused_device(): pl.pallas_call(functools.partial(fused_kernel, groups, capacity), out_sha...  143 us

profile of v4, /device:TPU:0, one launch (start us, length us, event | category | flops | bytes accessed | tf_op | source)
XLA Modules:
  0.0 144.5 jit_solution(5746657636690473789)
XLA Ops:
  0.6 143.0 %shard_map.86 = (bf16[128,1024]{1,0:T(8,128)(2,1)S(1)}, bf16[128,1024]{1,0:T(8,128)(2,1)S(1)}) custom-call(bf16[128,1024]{1,0:T(8,128)(2,1)} %tok_hbm.1, bf16[128,1024]{1,0:T(8,128)(2,1)} %cot_hbm.1, s32[8,128]{1,0:T(8,128)} %bitcast.2, f32[8,128]{1,0:T(8,128)} %bitcast.3, bf16[2,1024,768]{2,1,0:T(8,128)(2,1)} %wg_hbm.1, bf16[2,1024,768]{2,1,0:T(8,128)(2,1)} %wu_hbm.1, ...), custom_call_target="tpu_custom_call" | custom-call | tf_op jit(solution)/shard_map/pallas_call | solution.py:528
  143.7 0.8 shard_map.87

commit v5 on v4

--- a/solution.py
+++ b/solution.py
@@ -204,9 +204,14 @@
             cs.at[step, across, part], cr.at[step, across, part], at(core_peer),
         )
 
-    def y_copy(u, part, e):
+    spans = (((0, hid), (hid, 2 * hid)), ((0, hid),))
+
+    def y_copy(u, part, e, piece):
+        low, high = spans[part][piece]
+        here = (u, e, slice(None), slice(low, high))
         return copy(
-            ysend[part].at[u, e], yrecv[part].at[u, e], ys.at[u, part, e], yr.at[u, part, e], other_dp
+            ysend[part].at[here], yrecv[part].at[here],
+            ys.at[u, part, e, piece], yr.at[u, part, e, piece], other_dp,
         )
 
     def rc_copy(u, part):
@@ -316,7 +321,6 @@
         @pl.when(i == 0)
         def _():
             weight(0, 0).wait()
-            weight(1, 0).wait()
 
         @pl.when(i == 1)
         def _():
@@ -336,11 +340,19 @@
             def _():
                 mine = got[e * lines : (e + 1) * lines]
                 if part == 0:
-                    ysend_pre[u, e, :, :hid] = dot(mine, wg_ref[e], ((1,), (0,))).astype(BF16)
-                    ysend_pre[u, e, :, hid:] = dot(mine, wu_ref[e], ((1,), (0,))).astype(BF16)
+                    for piece, w_ref in enumerate((wg_ref, wu_ref)):
+                        low, high = spans[0][piece]
+                        if piece == 1 and e == 0:
+                            @pl.when(i == 0)
+                            def _():
+                                weight(1, 0).wait()
+
+                        value = dot(mine, w_ref[e], ((1,), (0,)))
+                        ysend_pre[u, e, :, low:high] = value.astype(BF16)
+                        y_copy(u, 0, e, piece).start()
                 else:
                     ysend_back[u, e] = dot(mine, wd_ref[e], ((1,), (1,))).astype(BF16)
-                y_copy(u, part, e).start()
+                    y_copy(u, 1, e, 0).start()
 
     def sums(u, e):
         def total(lo):
@@ -350,7 +362,8 @@
         return total(0), total(hid)
 
     def mixed_half(u, e, share):
-        y_copy(u, 0, e).wait_recv()
+        for piece in range(2):
+            y_copy(u, 0, e, piece).wait_recv()
         a, b = sums(u, e)
         act = (a * jax.nn.sigmoid(a) * b * share).astype(BF16)
         return dot(act, wd_ref[e], ((1,), (0,))).astype(BF16)
@@ -360,7 +373,7 @@
         sig = jax.nn.sigmoid(a)
         by_gate = b * sig * (1.0 + a * (1.0 - sig))
         by_up = a * sig
-        y_copy(u, 1, e).wait_recv()
+        y_copy(u, 1, e, 0).wait_recv()
         back = (ysend_back[u, e].astype(F32) + yrecv_back[u, e].astype(F32)) * share
         d_gate = (back * by_gate).astype(BF16)
         d_up = (back * by_up).astype(BF16)
@@ -486,7 +499,8 @@
                 rz_copy(step, part).wait_send()
         for u in range(units):
             for e in range(experts):
-                y_copy(u, part, e).wait_send()
+                for piece in range(len(spans[part])):
+                    y_copy(u, part, e, piece).wait_send()
         rc_copy(0, part).wait_send()
 
 
@@ -557,7 +571,7 @@
             dma((outer, 2)), dma((outer, 2)),
             dma((outer, 2)), dma((outer, 2)),
             dma((outer, 2, 2)), dma((outer, 2, 2)),
-            dma((units, 2, local_experts)), dma((units, 2, local_experts)),
+            dma((units, 2, local_experts, 2)), dma((units, 2, local_experts, 2)),
             dma((units, 2)), dma((units, 2)),
             dma((outer, 2)), dma((outer, 2)),
             dma((outer, 2)), dma((outer, 2)),

time: 145 us -> 145 us (level)
  no operation moved by 1% of the time
where the time goes in v5:
time: 145 us
  Pallas kernels  144 us (99%)
    pallas_call x1, Pallas kernels, fused_device(): pl.pallas_call(functools.partial(fused_kernel, groups, capacity), out_sha...  143 us

profile of v5, /device:TPU:0, one launch (start us, length us, event | category | flops | bytes accessed | tf_op | source)
XLA Modules:
  0.0 144.8 jit_solution(3463092170010139855)
XLA Ops:
  0.6 143.4 %shard_map.86 = (bf16[128,1024]{1,0:T(8,128)(2,1)S(1)}, bf16[128,1024]{1,0:T(8,128)(2,1)S(1)}) custom-call(bf16[128,1024]{1,0:T(8,128)(2,1)} %tok_hbm.1, bf16[128,1024]{1,0:T(8,128)(2,1)} %cot_hbm.1, s32[8,128]{1,0:T(8,128)} %bitcast.2, f32[8,128]{1,0:T(8,128)} %bitcast.3, bf16[2,1024,768]{2,1,0:T(8,128)(2,1)} %wg_hbm.1, bf16[2,1024,768]{2,1,0:T(8,128)(2,1)} %wu_hbm.1, ...), custom_call_target="tpu_custom_call" | custom-call | tf_op jit(solution)/shard_map/pallas_call | solution.py:542
  144.0 0.8 shard_map.87
